TPU v7x, 128 devices: a whole 4x4x4 slice. The times are simulated.
128 devices in a mesh: dp: 4 (over x_lo, core), ctx: 32 (over x_hi, y, z).
Axes of the slice: x: 4 (x_hi: 2, x_lo: 2; x = x_hi * 2 + x_lo), y: 4, z: 4, core: 2. Of those that a mesh axis runs over, the one named last changes fastest.
Arguments:
- frames: bfloat16 [4, 160, 16, 16, 512], P('dp', 'ctx'), may hold values from -6 to 6
- stream: bfloat16 [4, 160, 64, 3072], P('dp', 'ctx'), may hold values from -6 to 6
- video_frames: int32 [4], P('dp'), may hold values from 1 to 160
- conv_weight: bfloat16 [3, 3, 3, 512, 512], replicated, may hold values from -0.0546875 to 0.0546875
- latent_weight: bfloat16 [512, 16], replicated, may hold values from -0.25 to 0.25
- embed_weight: bfloat16 [64, 3072], replicated, may hold values from -0.75 to 0.75
- norm_gain: float32 [3072], replicated, may hold values from 0.25 to 1.75
- qkv_weight: bfloat16 [3072, 4608], P('ctx', 'dp'), may hold values from -0.109375 to 0.109375
Outputs:
- section: bfloat16 [4, 160, 16, 16, 512], P('dp', 'ctx')
- mixed: bfloat16 [4, 160, 64, 1536], P('dp', 'ctx')
All inputs are finite; a program needn't handle non-finite values.
Results may differ from a plain program's by a relative error of at most 0.0061.
Values may be sent and summed in bfloat16 or wider, within the bound.
A program may use at most 128 MiB of HBM per device.

v0:
```python
import jax
import jax.numpy as jnp
from jax import lax
from jax.sharding import Mesh
from jax.sharding import PartitionSpec as P

HD = 128
CTX = ("ctx_0", "ctx_1", "ctx_2")


def passed_along(value, axis, steps):
    count = lax.axis_size(axis)
    leading, last = (max(0, -steps), min(count, count - steps))
    return lax.ppermute(value, axis, [(source, source + steps) for source in range(leading, last)])


def from_everyone(array, axis):
    length = lax.axis_size(axis)
    return lax.all_to_all(
        jnp.broadcast_to(array[None], (length, *array.shape)), axis, 0, 0, tiled=True
    )


def laid_out(tiles, dim):
    dims = list(tiles.shape[1:])
    dims[dim] *= tiles.shape[0]
    return jnp.moveaxis(tiles, 0, dim).reshape(dims)


def gathered_copies(array, axis, dim):
    tiles = from_everyone(array, axis)
    return laid_out(tiles, dim)


def all_blocks(array, axes, turns):
    tiles = array[None]
    for k in turns:
        tiles = lax.all_gather(tiles, axes[k], axis=0, tiled=True)
    current = [lax.axis_size(axes[k]) for k in reversed(turns)]
    tiles = tiles.reshape(*current, *array.shape)
    turned = sorted(range(len(turns)), key=lambda place: turns[len(turns) - 1 - place])
    return tiles.transpose(*turned, *range(len(turns), tiles.ndim)).reshape(-1, *array.shape)


def gather_axes(array, axes, turns, dim):
    return laid_out(all_blocks(array, axes, turns), dim)


def attend(lengths, block):
    head_size = block.shape[-1] // 3
    slots = block.shape[1]
    query = block[..., 0:head_size]
    keys = block[..., head_size : 2 * head_size]
    values = block[..., 2 * head_size : 3 * head_size]
    scores = jnp.einsum(
        "gtphd,gsphd->gphts", query, keys, preferred_element_type=jnp.float32
    ) * head_size ** (-0.5)
    frame_ids = jnp.arange(slots, dtype=jnp.int32)
    video = frame_ids[None, :] < lengths[:, None]
    allowed = (
        video[:, :, None] & video[:, None, :] | (frame_ids[:, None] == frame_ids[None, :])[None]
    )
    scores = jnp.where(allowed[:, None, None], scores, -1e30)
    top = jnp.max(scores, axis=-1, keepdims=True)
    expo = jnp.exp(scores - top)
    probs = (expo / jnp.sum(expo, axis=-1, keepdims=True)).astype(jnp.bfloat16)
    out = jnp.einsum(
        "gphts,gsphd->gtphd", probs, values, preferred_element_type=jnp.float32
    ).astype(jnp.bfloat16)
    return lax.all_to_all(out, CTX, split_axis=1, concat_axis=2, tiled=True)


def on_device(
    frames, stream, video_frames, conv_weight, latent_weight, embed_weight, norm_gain, qkv_weight
):
    f_dev, height, width, channels = (
        frames.shape[1],
        frames.shape[2],
        frames.shape[3],
        frames.shape[4],
    )
    width_model = stream.shape[3]
    tokens_frame = stream.shape[2]
    act = jax.nn.silu(frames.astype(jnp.float32)).astype(jnp.bfloat16)
    past = passed_along(act[:, f_dev - 2 :], CTX, 1)
    joined = jnp.concatenate([past, act], axis=1)[0]
    padded = jnp.pad(joined, ((0, 0), (1, 1), (1, 1), (0, 0)))
    length = video_frames[0]
    frame_ids = lax.axis_index(CTX) * f_dev + jnp.arange(f_dev, dtype=jnp.int32)
    cells = f_dev * height * width
    total = jnp.zeros((cells, channels), jnp.float32)
    for lag in range(3):
        part = jnp.zeros((cells, channels), jnp.float32)
        for row in range(3):
            for col in range(3):
                slab = padded[
                    2 - lag : 2 - lag + f_dev, row : row + height, col : col + width, :
                ].reshape(-1, channels)
                part = part + jnp.dot(
                    slab, conv_weight[lag, row, col], preferred_element_type=jnp.float32
                )
        if lag == 0:
            total = part
        else:
            valid = ((frame_ids < length) & (frame_ids >= lag)).astype(jnp.float32)
            total = total + part * jnp.repeat(valid, height * width)[:, None]
    section = (frames.astype(jnp.float32) + total.reshape(frames.shape)).astype(jnp.bfloat16)
    latent = jnp.dot(
        section.reshape(-1, channels), latent_weight, preferred_element_type=jnp.float32
    ).astype(jnp.bfloat16)
    lat_size = latent.shape[1]
    latent = latent.reshape(f_dev, height // 2, 2, width // 2, 2, lat_size).transpose(
        0, 1, 3, 2, 4, 5
    )
    patches = latent.reshape(-1, 4 * lat_size)
    embedded = jnp.dot(patches, embed_weight, preferred_element_type=jnp.float32) + stream.reshape(
        -1, width_model
    ).astype(jnp.float32)
    scale = lax.rsqrt(jnp.mean(embedded * embedded, axis=-1, keepdims=True) + 1e-06)
    normed = (embedded * scale * norm_gain).astype(jnp.bfloat16)
    head_size = HD
    gathered, lengths = (
        gathered_copies(normed.reshape(1, -1, width_model), "dp", 0),
        gathered_copies(video_frames, "dp", 0),
    )
    group_count = gathered.shape[0]
    all_rows = gathered.reshape(-1, width_model)
    qkv = jnp.dot(
        all_rows, gather_axes(qkv_weight, CTX, (0, 1, 2), 0), preferred_element_type=jnp.float32
    )
    qkv = qkv.astype(jnp.bfloat16).reshape(
        group_count, f_dev, tokens_frame, qkv_weight.shape[1] // (3 * head_size), 3 * head_size
    )
    mixed = attend(lengths, lax.all_to_all(qkv, CTX, split_axis=2, concat_axis=1, tiled=True))
    mixed = lax.all_to_all(mixed, "dp", split_axis=0, concat_axis=3, tiled=True)
    return (section, mixed.reshape(1, f_dev, tokens_frame, -1))


def solution(mesh):
    finer = Mesh(mesh.devices.reshape(mesh.shape["dp"], 2, 4, 4), ("dp", "ctx_0", "ctx_1", "ctx_2"))
    return jax.shard_map(
        on_device,
        mesh=finer,
        in_specs=(
            P("dp", CTX, None, None, None),
            P("dp", CTX, None, None),
            P("dp"),
            P(),
            P(),
            P(),
            P(),
            P(CTX, "dp"),
        ),
        out_specs=(P("dp", CTX, None, None, None), P("dp", CTX, None, None)),
        check_vma=False,
    )
```

profile of v0, /device:TPU:1, one launch (start us, length us, event | category | flops | bytes accessed | tf_op | source)
XLA Modules:
  0.0 339.0 jit_solution(1459822168728964891)
XLA Ops:
  7.2 2.2 fusion.9
  9.5 4.4 %collective-permute-start = (bf16[1,2,16,16,512]{4,3,2,1,0:T(8,128)(2,1)S(1)}, bf16[1,2,16,16,512]{4,3,2,1,0:T(8,128)(2,1)S(1)}, u32[]{:S(2)}, u32[]{:S(2)}) collective-permute-start(bf16[1,2,16,16,512]{4,3,2,1,0:T(8,128)(2,1)S(1)} %slice.235), channel_id=1, source_target_pairs={{0,1},{1,2},{2,3},{3,4},{4,5},{5,6},{6,7},{7,8},{8,9},{9,10},{10,1... | collective-permute-start | bytes 1572872 | tf_op jit(solution)/shard_map/ppermute | solution.py:14
  13.9 8.3 %all-gather = bf16[192,1152]{1,0:T(8,128)(2,1)} all-gather(bf16[96,1152]{1,0:T(8,128)(2,1)S(1)} %copy-done.28), channel_id=2, replica_groups=mesh['dp'=4,'ctx_0'=2,'ctx_1'=4,'ctx_2'=4] {'ctx_0'}, dimensions={0}, use_global_device_ids=true | all-gather | bytes 663552 | tf_op jit(solution)/shard_map/all_gather | solution.py:38
  24.6 11.2 %pad_slice_fusion = (bf16[5,16,16,512]{3,2,1,0:T(8,128)(2,1)}, bf16[5,16,16,512]{3,2,1,0:T(8,128)(2,1)}, bf16[5,16,16,512]{3,2,1,0:T(8,128)(2,1)}, bf16[5,16,16,...) fusion(bf16[7,16,16,512]{3,2,1,0:T(8,128)(2,1)S(1)} %fusion.15), kind=kLoop, calls=%fused_computation.1 | loop fusion | bytes 26738688 | tf_op jit(solution)/shard_map/slice | solution.py:96
  35.8 4.0 %pad_slice_fusion.1 = (bf16[5,16,16,512]{3,2,1,0:T(8,128)(2,1)}, bf16[5,16,16,512]{3,2,1,0:T(8,128)(2,1)}, bf16[5,16,16,512]{3,2,1,0:T(8,128)(2,1)}, bf16[5,16,1...) fusion(bf16[7,16,16,512]{3,2,1,0:T(8,128)(2,1)S(1)} %fusion.15), kind=kLoop, calls=%fused_computation.2 | loop fusion | bytes 8388608 | tf_op jit(solution)/shard_map/slice | solution.py:96
  51.0 2.3 convolution_add_fusion.17
  63.5 2.4 convolution_add_fusion.10
  68.1 2.4 convolution_add_fusion.6
  70.5 2.2 convolution_add_fusion.5
  88.0 4.3 %broadcast_in_dim.20 = bf16[4,1,320,3072]{3,2,1,0:T(8,128)(2,1)} broadcast(bf16[320,3072]{1,0:T(8,128)(2,1)S(1)} %multiply_convert_fusion), dimensions={2,3} | broadcast | bytes 9830400 | tf_op jit(solution)/shard_map/broadcast_in_dim | solution.py:20
  92.2 6.9 %all-to-all-start = ((bf16[4,1,320,3072]{3,2,1,0:T(8,128)(2,1)}), bf16[4,1,320,3072]{3,2,1,0:T(8,128)(2,1)}, u32[]{:S(2)}, u32[]{:S(2)}) async-start(bf16[4,1,320,3072]{3,2,1,0:T(8,128)(2,1)} %broadcast_in_dim.20), calls=%async_computation | async-start | bytes 15728640 | tf_op jit(solution)/shard_map/all_to_all | solution.py:19
  99.2 50.4 %all-gather.6.cloned.1.call-done = bf16[32,96,1152]{2,1,0:T(8,128)(2,1)} async-done(((bf16[8,96,1152]{2,1,0:T(8,128)(2,1)}), bf16[32,96,1152]{2,1,0:T(8,128)(2,1)}) %all-gather.6.cloned.1.call-update) | async-done | bytes 7077904 | tf_op jit(solution)/shard_map/all_gather | solution.py:38
  149.5 6.7 %copy.61 = bf16[2,4,4,96,1152]{4,3,2,1,0:T(8,128)(2,1)} copy(bf16[2,4,4,96,1152]{4,3,0,1,2:T(8,128)(2,1)} %bitcast.178) | data formatting | bytes 14155776 | tf_op jit(solution)/shard_map/transpose | solution.py:42
  156.3 29.5 %all-to-all-done = bf16[4,1,320,3072]{3,2,1,0:T(8,128)(2,1)} async-done(((bf16[4,1,320,3072]{3,2,1,0:T(8,128)(2,1)}), bf16[4,1,320,3072]{3,2,1,0:T(8,128)(2,1)}, u32[]{:S(2)}, u32[]{:S(2)}) %all-to-all-start) | async-done | bytes 7864352 | tf_op jit(solution)/shard_map/all_to_all | solution.py:19
  186.3 4.4 %all-to-all-start.2 = ((s32[4,1,1]{2,1,0:T(1,128)}), s32[4,1,1]{2,1,0:T(1,128)S(1)}, u32[]{:S(2)}, u32[]{:S(2)}) async-start(s32[4,1,1]{2,1,0:T(1,128)} %broadcast_in_dim.22), calls=%async_computation.2 | async-start | bytes 4096 | tf_op jit(solution)/shard_map/all_to_all | solution.py:19
  190.7 14.7 %convolution_convert_fusion = bf16[1280,1152]{1,0:T(8,128)(2,1)S(1)} fusion(bf16[1280,3072]{1,0:T(8,128)(2,1)} %bitcast.61, bf16[3072,1152]{1,0:T(8,128)(2,1)} %bitcast.179), kind=kOutput, calls=%fused_computation.25 | convolution fusion | flops 9061171200 | bytes 17891328 | tf_op jit(solution)/shard_map/dot_general | solution.py:128
  205.4 4.3 %reshape.226 = bf16[4,5,64,3,384]{4,3,2,1,0:T(4,128)(2,1)} reshape(bf16[1280,1152]{1,0:T(8,128)(2,1)S(1)} %convolution_convert_fusion) | data formatting | bytes 5898240 | tf_op jit(solution)/shard_map/reshape | solution.py:131
  209.8 7.5 %copy.62 = bf16[4,5,64,3,384]{4,0,3,1,2:T(4,128)(2,1)} copy(bf16[4,5,64,3,384]{4,3,2,1,0:T(4,128)(2,1)} %reshape.226) | data formatting | bytes 5898240 | tf_op jit(solution)/shard_map/reshape | solution.py:131
  217.3 17.6 %all-to-all-start.1 = ((bf16[4,5,64,3,384]{4,0,3,1,2:T(4,128)(2,1)}), bf16[4,5,64,3,384]{4,0,3,1,2:T(4,128)(2,1)S(1)}, u32[]{:S(2)}, u32[]{:S(2)}) async-start(bf16[4,5,64,3,384]{4,0,3,1,2:T(4,128)(2,1)} %copy.62), calls=%async_computation.1 | async-start | bytes 5898240 | tf_op jit(solution)/shard_map/all_to_all | solution.py:134
  235.3 37.3 %all-to-all-done.1 = bf16[4,5,64,3,384]{4,0,3,1,2:T(4,128)(2,1)S(1)} async-done(((bf16[4,5,64,3,384]{4,0,3,1,2:T(4,128)(2,1)}), bf16[4,5,64,3,384]{4,0,3,1,2:T(4,128)(2,1)S(1)}, u32[]{:S(2)}, u32[]{:S(2)}) %all-to-all-start.1) | async-done | bytes 2949152 | tf_op jit(solution)/shard_map/all_to_all | solution.py:134
  272.7 2.3 copy.63
  274.9 2.1 fusion.83
  281.0 25.4 %all_to_all.62 = bf16[4,160,2,3,128]{4,0,3,2,1:T(4,128)(2,1)S(1)} all-to-all(bf16[4,160,2,3,128]{4,0,3,2,1:T(4,128)(2,1)S(1)} %copy.68), channel_id=1, replica_groups=mesh['dp'=4,'ctx_0'=2,'ctx_1'=4,'ctx_2'=4] {'ctx_0','ctx_1','ctx_2'}, dimensions={1} | all-to-all | bytes 1966080 | tf_op jit(solution)/shard_map/all_to_all | solution.py:70
  308.2 21.2 %all_to_all.63 = bf16[4,5,64,3,128]{4,2,3,1,0:T(8,128)(2,1)S(1)} all-to-all(bf16[4,5,64,3,128]{4,2,3,1,0:T(8,128)(2,1)S(1)} %bitcast.208), channel_id=1, replica_groups=mesh['dp'=4,'ctx_0'=2,'ctx_1'=4,'ctx_2'=4] {'dp'}, dimensions={0} | all-to-all | bytes 1966080 | tf_op jit(solution)/shard_map/all_to_all | solution.py:135
  (130 shorter events, 49.4 us)
Async XLA Ops:
  7.2 79.4 %copy-start = (bf16[64,3072]{1,0:T(8,128)(2,1)S(1)}, bf16[64,3072]{1,0:T(8,128)(2,1)}, u32[]{:S(2)}) copy-start(bf16[64,3072]{1,0:T(8,128)(2,1)} %param.13) | copy-start | bytes 1179652
  7.2 6.7 %copy-start.28 = (bf16[96,1152]{1,0:T(8,128)(2,1)S(1)}, bf16[96,1152]{1,0:T(8,128)(2,1)}, u32[]{:S(2)}) copy-start(bf16[96,1152]{1,0:T(8,128)(2,1)} %param.15) | copy-start | bytes 663556
  7.2 60.8 %all-gather.4.cloned.1.call-start = ((), (), s32[]{:S(2)}) async-start(), calls=%async_computation.5 | async-start | bytes 2211840 | tf_op jit(solution)/shard_map/all_gather | solution.py:38
  9.5 15.0 %collective-permute-start = (bf16[1,2,16,16,512]{4,3,2,1,0:T(8,128)(2,1)S(1)}, bf16[1,2,16,16,512]{4,3,2,1,0:T(8,128)(2,1)S(1)}, u32[]{:S(2)}, u32[]{:S(2)}) collective-permute-start(bf16[1,2,16,16,512]{4,3,2,1,0:T(8,128)(2,1)S(1)} %slice.235), channel_id=1, source_target_pairs={{0,1},{1,2},{2,3},{3,4},{4,5},{5,6},{6,7},{7,8},{8,9},{9,10},{10,1... | collective-permute-start | bytes 1572872 | tf_op jit(solution)/shard_map/ppermute | solution.py:14
  22.2 127.3 %all-gather.6.cloned.1.call-start = ((), (), s32[]{:S(2)}) async-start(), calls=%async_computation.6 | async-start | bytes 8847360 | tf_op jit(solution)/shard_map/all_gather | solution.py:38
  24.4 15.4 %slice-start = ((s8[14155776]{0:T(1024)(128)(4,1)}), s8[4194304]{0:T(1024)(128)(4,1)S(1)}, s32[]{:S(2)}) async-start(s8[14155776]{0:T(1024)(128)(4,1)} %bitcast.173), calls=%async_computation.7 | async-start | bytes 8388608
  24.6 15.3 %slice-start.1 = ((s8[14155776]{0:T(1024)(128)(4,1)}), s8[4194304]{0:T(1024)(128)(4,1)S(1)}, s32[]{:S(2)}) async-start(s8[14155776]{0:T(1024)(128)(4,1)} %bitcast.173), calls=%async_computation.8 | async-start | bytes 8388608
  24.6 15.3 %slice-start.2 = ((s8[14155776]{0:T(1024)(128)(4,1)}), s8[4194304]{0:T(1024)(128)(4,1)S(1)}, s32[]{:S(2)}) async-start(s8[14155776]{0:T(1024)(128)(4,1)} %bitcast.173), calls=%async_computation.9 | async-start | bytes 8388608
  24.6 15.3 %slice-start.3 = ((s8[14155776]{0:T(1024)(128)(4,1)}), s8[1572864]{0:T(1024)(128)(4,1)S(1)}, s32[]{:S(2)}) async-start(s8[14155776]{0:T(1024)(128)(4,1)} %bitcast.173), calls=%async_computation.10 | async-start | bytes 3145728
  51.0 2.4 copy-start.10
  68.1 2.4 copy-start.23
  70.5 2.2 copy-start.26
  72.7 2.0 copy-start.25
  74.7 2.0 copy-start.24
  76.7 2.1 copy-start.2
  76.7 2.7 copy-start.3
  76.8 3.0 copy-start.20
  79.8 2.0 copy-start.19
  81.8 2.0 copy-start.21
  84.4 2.2 copy-start.27
  92.2 93.5 %all-to-all-start = ((bf16[4,1,320,3072]{3,2,1,0:T(8,128)(2,1)}), bf16[4,1,320,3072]{3,2,1,0:T(8,128)(2,1)}, u32[]{:S(2)}, u32[]{:S(2)}) async-start(bf16[4,1,320,3072]{3,2,1,0:T(8,128)(2,1)} %broadcast_in_dim.20), calls=%async_computation | async-start | bytes 15728640 | tf_op jit(solution)/shard_map/all_to_all | solution.py:19
  186.3 31.0 %all-to-all-start.2 = ((s32[4,1,1]{2,1,0:T(1,128)}), s32[4,1,1]{2,1,0:T(1,128)S(1)}, u32[]{:S(2)}, u32[]{:S(2)}) async-start(s32[4,1,1]{2,1,0:T(1,128)} %broadcast_in_dim.22), calls=%async_computation.2 | async-start | bytes 4096 | tf_op jit(solution)/shard_map/all_to_all | solution.py:19
  217.3 55.3 %all-to-all-start.1 = ((bf16[4,5,64,3,384]{4,0,3,1,2:T(4,128)(2,1)}), bf16[4,5,64,3,384]{4,0,3,1,2:T(4,128)(2,1)S(1)}, u32[]{:S(2)}, u32[]{:S(2)}) async-start(bf16[4,5,64,3,384]{4,0,3,1,2:T(4,128)(2,1)} %copy.62), calls=%async_computation.1 | async-start | bytes 5898240 | tf_op jit(solution)/shard_map/all_to_all | solution.py:134
  308.2 23.7 %copy-start.1 = (bf16[64,3072]{1,0:T(8,128)(2,1)S(1)}, bf16[64,3072]{1,0:T(8,128)(2,1)}, u32[]{:S(2)}) copy-start(bf16[64,3072]{1,0:T(8,128)(2,1)} %param.13) | copy-start | bytes 1179652
  (17 other events, 22.1 us)
Sparse Core Ops, SparseCore 0:
  22.3 38.4 all-gather.3
  68.2 81.2 all-gather.5
where the time goes:
time: 344 us; the launch traced here: 339 us
  waiting for transfers between devices  119 us (35%)
  local copies, waits for them, and re-layouts  57.7 us (17%)
  blocking collectives  54.9 us (16%)
  matrix products  52.3 us (15%)
  starting transfers between devices  33.3 us (10%)
  between operations  15.6 us (5%)
  other arithmetic  6.67 us (2%)
    all_gather x2, waiting for transfers between devices, all_blocks(): tiles = lax.all_gather(tiles, axes[k], axis=0, tiled=True)  50.4 us
    all_to_all x1, waiting for transfers between devices, on_device(): lax.all_to_all(qkv, CTX, split_axis=2, concat_axis=1, tiled=True)  37.3 us
    dot_general x27, matrix products, on_device(): jnp.dot(slab, conv_weight[lag, row, col], preferred_element_type=jnp.floa...  34.6 us
    all_to_all x2, waiting for transfers between devices, from_everyone(): lax.all_to_all(jnp.broadcast_to(array[None], (length, *array.shape)), axi...  29.5 us
    all_to_all x1, blocking collectives, attend(): return lax.all_to_all(out, CTX, split_axis=1, concat_axis=2, tiled=True)  25.4 us
    all_to_all x1, blocking collectives, on_device(): mixed = lax.all_to_all(mixed, 'dp', split_axis=0, concat_axis=3, tiled=True)  21.2 us
    all_to_all x1, starting transfers between devices, on_device(): lax.all_to_all(qkv, CTX, split_axis=2, concat_axis=1, tiled=True)  17.6 us
    slice x2, local copies, waits for them, and re-layouts, on_device(): padded[2 - lag:2 - lag + f_dev, row:row + height, col:col + width, :]  15.2 us
  transfers between devices with their start and end apart: 6, of which 4 were waited for; matrix products, arithmetic and copies ran while one was open for 27% of the time, Pallas kernels for 0%

commit v1 on v0

v1 whole, which is shorter than its diff:
```python
import functools

import jax
import jax.numpy as jnp
from jax import lax
from jax.experimental import pallas as pl
from jax.experimental.pallas import tpu as pltpu
from jax.sharding import Mesh
from jax.sharding import PartitionSpec as P

AXES = ("xl", "co", "xh", "y", "z")
CTX = ("xh", "y", "z")
MESH = pl.DeviceIdType.MESH
F32 = jnp.float32
BF16 = jnp.bfloat16
NCTX = 32
LANES = 128


def place():
    return {a: lax.axis_index(a) for a in AXES}


def ctx_of(me):
    return (me["xh"] * 4 + me["y"]) * 4 + me["z"]


def at_ctx(me, c, co=None):
    return (me["xl"], me["co"] if co is None else co, c // 16, (c // 4) % 4, c % 4)


def coordinate(me, axis):
    return (me["xh"] * 2 + me["xl"], me["y"], me["z"])[axis]


def moved(me, axis, c):
    if axis == 0:
        return (c % 2, me["co"], c // 2, me["y"], me["z"])
    if axis == 1:
        return (me["xl"], me["co"], me["xh"], c, me["z"])
    return (me["xl"], me["co"], me["xh"], me["y"], c)


def gather_copies(me, wall, ssem, rsem):
    rows = wall.shape[4] // 3
    half = rows // 2
    stages = [[] for _ in range(6)]
    for part in range(3):
        for phase in range(3):
            axis = (part + phase) % 3
            full = [(part + i) % 3 for i in range(phase)]
            c = coordinate(me, axis)
            for step in range(2):
                for way in range(2):
                    sign = 1 - 2 * way
                    to = (c + sign + 4) % 4
                    held = c if step == 0 else (c - sign + 4) % 4
                    begin = part * rows + (half if step and way else 0)
                    size = half if step else rows
                    index = []
                    for a in range(3):
                        if a in full:
                            got = None
                        elif a == axis:
                            got = held
                        else:
                            got = coordinate(me, a)
                        if a == 0:
                            if got is None:
                                index += [pl.ds(0, 2), pl.ds(0, 2)]
                            else:
                                index += [got % 2, got // 2]
                        else:
                            index.append(pl.ds(0, 4) if got is None else got)
                    block = wall.at[(*index, pl.ds(begin, size))]
                    n = ((part * 3 + phase) * 2 + step) * 2 + way
                    stages[phase * 2 + step].append(
                        pltpu.make_async_remote_copy(
                            src_ref=block,
                            dst_ref=block,
                            send_sem=ssem.at[n],
                            recv_sem=rsem.at[n],
                            device_id=moved(me, axis, to),
                            device_id_type=MESH,
                        )
                    )
    return stages


def section_kernel(
    frames, stream, length, cw, lw4, ew, gain, w,
    sec_out, wall, xr,
    xin, xcat, cwv, acc, secb, strm, nt, sb, sent,
    cw_sem, in_sem, w_ssem, w_rsem, h_ssem, h_rsem, a_ssem, a_rsem, out_sem, own_sem,
):
    me = place()
    ctx = ctx_of(me)
    mine = wall.at[me["xl"], me["xh"], me["y"], me["z"]]
    place_w = pltpu.make_async_copy(w, mine, own_sem.at[0])
    place_w.start()
    load_frames = pltpu.make_async_copy(frames, xin.at[pl.ds(2, 5)], in_sem.at[0])
    load_frames.start()

    def load_cw(s):
        return pltpu.make_async_copy(cw.at[s], cwv.at[s], cw_sem.at[s])

    def order(k):
        return (2 - k // 3) * 3 + k % 3

    for k in range(9):
        load_cw(order(k)).start()
    load_stream = pltpu.make_async_copy(stream, strm, in_sem.at[1])
    load_stream.start()

    barrier = pltpu.get_barrier_semaphore()

    @pl.loop(1, NCTX)
    def _(k):
        pl.semaphore_signal(
            barrier, inc=1, device_id=at_ctx(me, (ctx + k) % NCTX), device_id_type=MESH
        )

    x = coordinate(me, 0)
    for d in (1, 3):
        pl.semaphore_signal(
            barrier, inc=1, device_id=moved(me, 0, (x + d) % 4), device_id_type=MESH
        )
    pl.semaphore_wait(barrier, NCTX + 1)

    halo = pltpu.make_async_remote_copy(
        src_ref=frames.at[pl.ds(3, 2)],
        dst_ref=xin.at[pl.ds(0, 2)],
        send_sem=h_ssem,
        recv_sem=h_rsem,
        device_id=at_ctx(me, (ctx + 1) % NCTX),
        device_id_type=MESH,
    )
    halo.start()
    place_w.wait()
    stages = gather_copies(me, wall, w_ssem, w_rsem)

    def start_stage(k):
        if k:
            for copy in stages[k - 1]:
                copy.wait_recv()
        for copy in stages[k]:
            copy.start()

    start_stage(0)

    edge = jnp.zeros((7, 1, 16, 1536), BF16)
    xcat[:, pl.ds(0, 1)] = edge
    xcat[:, pl.ds(17, 1)] = edge
    column = lax.broadcasted_iota(jnp.int32, (256, 512), 0) & 15

    def spread(i, factor):
        v = xin[i].astype(F32)
        act = (v / (1.0 + jnp.exp(-v))).astype(BF16).astype(F32) * factor
        before = jnp.where(column == 0, 0.0, pltpu.roll(act, 1, 0))
        after = jnp.where(column == 15, 0.0, pltpu.roll(act, 255, 0))
        for b, part in enumerate((before, act, after)):
            xcat[i, pl.ds(1, 16), :, pl.ds(512 * b, 512)] = part.astype(BF16).reshape(16, 16, 512)

    load_frames.wait()

    @pl.loop(2, 7)
    def _(i):
        spread(i, 1.0)

    cell = lax.broadcasted_iota(jnp.int32, (256, 64), 0)
    lane = lax.broadcasted_iota(jnp.int32, (256, 64), 1)
    corner = ((cell >> 4) & 1) * 2 + (cell & 1)
    keep = jnp.where((lane >> 4) == corner, 1.0, 0.0)
    tok = lax.broadcasted_iota(jnp.int32, (64, 256), 0)
    cel = lax.broadcasted_iota(jnp.int32, (64, 256), 1)
    pick = jnp.where((cel >> 5) * 8 + ((cel & 15) >> 1) == tok, 1.0, 0.0).astype(BF16)
    count = length[0]

    def conv(first, many, checkpoints, arrive):
        acc[pl.ds(0, many * 256)] = jnp.zeros((many * 256, 512), F32)

        @pl.loop(0, 9)
        def _(k):
            if arrive:
                load_cw(order(k)).wait()
            for when, stage in checkpoints:
                @pl.when(k == when)
                def _():
                    start_stage(stage)

            @pl.when(k == 6)
            def _():
                for f in range(many):
                    video = jnp.where(ctx * 5 + first + f < count, 1.0, 0.0)
                    acc[pl.ds(f * 256, 256)] = acc[pl.ds(f * 256, 256)] * video

            lag = 2 - k // 3
            slab = xcat[pl.ds(first + 2 - lag, many), pl.ds(k % 3, 16)]
            acc[pl.ds(0, many * 256)] += jnp.dot(
                slab.reshape(many * 256, 1536), cwv[order(k)], preferred_element_type=F32
            )

    def finish(first, many, n):
        @pl.loop(0, many)
        def _(i):
            t = first + i
            sec = (xin[t + 2].astype(F32) + acc[pl.ds(pl.multiple_of(i * 256, 256), 256)]).astype(BF16)
            secb[t] = sec
            lat = jnp.dot(sec, lw4[...], preferred_element_type=F32).astype(BF16).astype(F32)
            patches = jnp.dot(pick, (lat * keep).astype(BF16), preferred_element_type=F32).astype(BF16)
            e = jnp.dot(patches, ew[...], preferred_element_type=F32) + strm[t].astype(F32)
            scale = lax.rsqrt(jnp.mean(e * e, axis=-1, keepdims=True) + 1e-06)
            e = e * scale * gain[...]
            for j in range(24):
                nt[pl.ds(j, 64, stride=24), :] = e[:, j * LANES : (j + 1) * LANES]
            sb[t] = nt[...].astype(BF16).reshape(32, 48, LANES)

        span = pl.ds(first, many)
        pltpu.make_async_copy(secb.at[span], sec_out.at[span], out_sem.at[n]).start()
        stage = pltpu.make_async_copy(sb.at[span], sent.at[span], own_sem.at[1 + n])
        stage.start()
        stage.wait()

        @pl.loop(1, NCTX)
        def _(k):
            to = (ctx + k) % NCTX
            pltpu.make_async_remote_copy(
                src_ref=sent.at[span, to],
                dst_ref=xr.at[ctx, span],
                send_sem=a_ssem.at[n],
                recv_sem=a_rsem.at[n],
                device_id=at_ctx(me, to),
                device_id_type=MESH,
            ).start()

        pltpu.make_async_copy(sent.at[span, ctx], xr.at[ctx, span], own_sem.at[3 + n]).start()

    conv(2, 3, ((2, 1), (5, 2)), True)
    start_stage(3)
    load_stream.wait()
    finish(2, 3, 0)
    halo.wait_recv()
    inner = jnp.where(ctx > 0, 1.0, 0.0)

    @pl.loop(0, 2)
    def _(i):
        spread(i, inner)

    conv(0, 2, ((3, 4),), False)
    finish(0, 2, 1)
    start_stage(5)
    for copy in stages[5]:
        copy.wait_recv()
    for stage in stages:
        for copy in stage:
            copy.wait_send()
    halo.wait_send()
    for n, (first, many) in enumerate(((2, 3), (0, 2))):
        span = pl.ds(first, many)
        bulk = xr.at[pl.ds(0, NCTX - 1), span]
        pltpu.make_async_copy(bulk, bulk, a_rsem.at[n]).wait()
        pltpu.make_async_copy(bulk, bulk, a_ssem.at[n]).wait()
        pltpu.make_async_copy(sent.at[span, ctx], xr.at[ctx, span], own_sem.at[3 + n]).wait()
        pltpu.make_async_copy(secb.at[span], sec_out.at[span], out_sem.at[n]).wait()


def sections(frames, stream, length, cw, lw4, ew, gain, w):
    hbm = pl.BlockSpec(memory_space=pl.ANY)
    vmem = pl.BlockSpec(memory_space=pltpu.VMEM)
    smem = pl.BlockSpec(memory_space=pltpu.SMEM)
    dma = pltpu.SemaphoreType.DMA
    return pl.pallas_call(
        section_kernel,
        out_shape=(
            jax.ShapeDtypeStruct((5, 256, 512), BF16),
            jax.ShapeDtypeStruct((2, 2, 4, 4, 96, 1152), BF16),
            jax.ShapeDtypeStruct((NCTX, 5, 48, LANES), BF16),
        ),
        in_specs=[hbm, hbm, smem, hbm, vmem, vmem, vmem, vmem],
        out_specs=(hbm, hbm, hbm),
        scratch_shapes=[
            pltpu.VMEM((7, 256, 512), BF16),
            pltpu.VMEM((7, 18, 16, 1536), BF16),
            pltpu.VMEM((9, 1536, 512), BF16),
            pltpu.VMEM((768, 512), F32),
            pltpu.VMEM((5, 256, 512), BF16),
            pltpu.VMEM((5, 64, 3072), BF16),
            pltpu.VMEM((1536, LANES), F32),
            pltpu.VMEM((5, 32, 48, LANES), BF16),
            pltpu.VMEM((5, 32, 48, LANES), BF16),
            dma((9,)), dma((2,)), dma((36,)), dma((36,)), dma, dma, dma((2,)), dma((2,)), dma((2,)), dma((5,)),
        ],
        compiler_params=pltpu.CompilerParams(
            collective_id=0, has_side_effects=True, vmem_limit_bytes=60 * 2**20
        ),
        name="sections",
    )(frames, stream, length, cw, lw4, ew, gain, w)


def attention_kernel(
    wall, xr, lens, out,
    wv, xs, lsib, xf, xm, qs, of, osd, sent, orr, off, outf,
    w_sem, x_ssem, x_rsem, o_ssem, o_rsem, own_sem,
):
    me = place()
    ctx = ctx_of(me)
    co = me["co"]

    def load_w(h):
        return pltpu.make_async_copy(
            wall.at[h // 3, :, pl.ds(pl.multiple_of((h % 3) * 384, 128), 384)], wv.at[h], w_sem.at[h]
        )

    for h in range(6):
        load_w(h).start()

    barrier = pltpu.get_barrier_semaphore()

    @pl.loop(1, NCTX)
    def _(k):
        pl.semaphore_signal(
            barrier, inc=1, device_id=at_ctx(me, (ctx + k) % NCTX), device_id_type=MESH
        )

    @pl.loop(0, NCTX)
    def _(k):
        pl.semaphore_signal(
            barrier, inc=1, device_id=at_ctx(me, (ctx + k) % NCTX, 1 - co), device_id_type=MESH
        )

    pl.semaphore_wait(barrier, 2 * NCTX - 1)
    swaps = [
        pltpu.make_async_remote_copy(
            src_ref=a,
            dst_ref=b,
            send_sem=x_ssem.at[n],
            recv_sem=x_rsem.at[n],
            device_id=at_ctx(me, ctx, 1 - co),
            device_id_type=MESH,
        )
        for n, (a, b) in enumerate(((xr, xs), (lens, lsib)))
    ]
    for copy in swaps:
        copy.start()

    row = lax.broadcasted_iota(jnp.int32, (160, 160), 0)
    col = lax.broadcasted_iota(jnp.int32, (160, 160), 1)
    row_frame = (row & 31) * 5 + (row >> 5)
    col_frame = (col & 31) * 5 + (col >> 5)
    same = row == col

    for g in range(2):
        if g:
            for copy in swaps:
                copy.wait_recv()
        src, lref = ((xr, lens), (xs, lsib))[g]
        xf[...] = src[...].astype(F32)
        for f in range(5):
            for pos in range(2):
                for j in range(24):
                    xm[pl.ds(pos * 160 + f * 32, 32), pl.ds(j * LANES, LANES)] = xf[
                        pl.ds((f * 2 + pos) * 24 + j, 32, stride=240), :
                    ].astype(BF16)
        most = jnp.broadcast_to(lref[0:1, 0:1], (160, 160))
        allowed = ((row_frame < most) & (col_frame < most)) | same

        @pl.loop(0, 6)
        def _(h):
            if g == 0:
                load_w(h).wait()
            qs[...] = jnp.dot(xm[...], wv[h], preferred_element_type=F32).astype(BF16)
            for pos in range(2):
                rows = pl.ds(pos * 160, 160)
                scores = lax.dot_general(
                    qs[rows, 0:128], qs[rows, 128:256], (((1,), (1,)), ((), ())),
                    preferred_element_type=F32,
                ) * (128.0 ** -0.5)
                scores = jnp.where(allowed, scores, -1e30)
                expo = jnp.exp(scores - jnp.max(scores, axis=-1, keepdims=True))
                probs = (expo / jnp.sum(expo, axis=-1, keepdims=True)).astype(BF16)
                o = jnp.dot(probs, qs[rows, 256:384], preferred_element_type=F32)
                for f in range(5):
                    of[pl.ds(f * 12 + pos * 6 + h, 32, stride=64), :] = o[f * 32 : (f + 1) * 32]

        osd[g] = of[...].astype(BF16).reshape(NCTX, 64, LANES)
        stage = pltpu.make_async_copy(osd.at[g], sent.at[g], own_sem.at[g])
        stage.start()
        stage.wait()

        @pl.loop(1 - g, NCTX)
        def _(k):
            to = (ctx + k) % NCTX
            pltpu.make_async_remote_copy(
                src_ref=sent.at[g, to],
                dst_ref=orr.at[co, ctx],
                send_sem=o_ssem.at[g],
                recv_sem=o_rsem.at[g],
                device_id=at_ctx(me, to, co if g == 0 else 1 - co),
                device_id_type=MESH,
            ).start()

        if g == 0:
            pltpu.make_async_copy(sent.at[0, ctx], orr.at[co, ctx], own_sem.at[2]).start()

    pltpu.make_async_copy(sent.at[0, ctx], orr.at[co, ctx], own_sem.at[2]).wait()
    for copy in swaps:
        copy.wait_send()
    for g in range(2):
        bulk = orr.at[0, pl.ds(0, NCTX - 1 + g)]
        pltpu.make_async_copy(bulk, bulk, o_rsem.at[g]).wait()
        pltpu.make_async_copy(bulk, bulk, o_ssem.at[g]).wait()
    off[...] = orr[...].astype(F32).reshape(2 * NCTX * 64, LANES)
    for c in range(2):
        for h in range(6):
            head = 6 * (h // 3) + 3 * c + h % 3
            for f in range(5):
                for pos in range(2):
                    outf[pl.ds(head * 320 + f * 64 + pos, 32, stride=2), :] = off[
                        pl.ds(c * 2048 + f * 12 + pos * 6 + h, 32, stride=64), :
                    ]
    for head in range(12):
        out[:, pl.ds(head * LANES, LANES)] = outf[pl.ds(head * 320, 320)].astype(BF16)


def attention(wall, xr, lens):
    hbm = pl.BlockSpec(memory_space=pl.ANY)
    vmem = pl.BlockSpec(memory_space=pltpu.VMEM)
    dma = pltpu.SemaphoreType.DMA
    return pl.pallas_call(
        attention_kernel,
        out_shape=jax.ShapeDtypeStruct((320, 1536), BF16),
        in_specs=[hbm, vmem, vmem],
        out_specs=vmem,
        scratch_shapes=[
            pltpu.VMEM((6, 3072, 384), BF16),
            pltpu.VMEM((7680, LANES), BF16),
            pltpu.VMEM((8, LANES), jnp.int32),
            pltpu.VMEM((7680, LANES), F32),
            pltpu.VMEM((320, 3072), BF16),
            pltpu.VMEM((320, 384), BF16),
            pltpu.VMEM((2048, LANES), F32),
            pltpu.VMEM((2, NCTX, 64, LANES), BF16),
            pltpu.VMEM((2, NCTX, 64, LANES), BF16),
            pltpu.VMEM((2, NCTX, 64, LANES), BF16),
            pltpu.VMEM((4096, LANES), F32),
            pltpu.VMEM((3840, LANES), F32),
            dma((6,)), dma((2,)), dma((2,)), dma((2,)), dma((2,)), dma((3,)),
        ],
        compiler_params=pltpu.CompilerParams(
            collective_id=1, has_side_effects=True, vmem_limit_bytes=60 * 2**20
        ),
        name="attention",
    )(wall, xr, lens)


def on_device(frames, stream, video_frames, conv_weight, latent_weight, embed_weight, norm_gain, qkv_weight):
    section, wall, xr = sections(
        frames.reshape(5, 256, 512),
        stream.reshape(5, 64, 3072),
        video_frames,
        conv_weight.reshape(9, 1536, 512),
        jnp.tile(latent_weight, (1, 4)),
        embed_weight,
        norm_gain.reshape(1, 3072),
        qkv_weight,
    )
    lens = jnp.broadcast_to(video_frames[0], (8, LANES))
    mixed = attention(wall.reshape(2, 3072, 1152), xr.reshape(7680, LANES), lens)
    return section.reshape(frames.shape), mixed.reshape(1, 5, 64, 1536)


def solution(mesh):
    finer = Mesh(mesh.devices.reshape(2, 2, 2, 4, 4), AXES)
    dp = ("xl", "co")
    return jax.shard_map(
        on_device,
        mesh=finer,
        in_specs=(
            P(dp, CTX, None, None, None),
            P(dp, CTX, None, None),
            P(dp),
            P(),
            P(),
            P(),
            P(),
            P(CTX, dp),
        ),
        out_specs=(P(dp, CTX, None, None, None), P(dp, CTX, None, None)),
        check_vma=False,
    )
```

time: 344 us -> 155 us (0.45); the launches traced: 339 us -> 155 us
  Pallas kernels: 0 us -> 149 us
  waiting for transfers between devices: 119 us -> 0 us
  blocking collectives: 54.9 us -> 0 us
  local copies, waits for them, and re-layouts: 57.7 us -> 4.69 us
  matrix products: 52.3 us -> 0 us
  starting transfers between devices: 33.3 us -> 0 us
  between operations: 15.6 us -> 1.31 us
  other arithmetic: 6.67 us -> 0 us
    pallas_call x0 -> x2, Pallas kernels: none -> 149 us  [the longest x1 103 us: sections(): pl.pallas_call(section_kernel, out_shape=(jax.ShapeDtypeStruct((5, 256, 5...]
    all_to_all x3 -> x0, waiting for transfers between devices: 66.8 us -> none  [the longest x1 37.3 us: on_device(): lax.all_to_all(qkv, CTX, split_axis=2, concat_axis=1, tiled=True)]
    dot_general x32 -> x0, matrix products: 52.3 us -> none  [the longest x27 34.6 us: on_device(): jnp.dot(slab, conv_weight[lag, row, col], preferred_element_type=jnp.floa...]
    all_gather x2 -> x0, waiting for transfers between devices: 50.4 us -> none  [all_blocks(): tiles = lax.all_gather(tiles, axes[k], axis=0, tiled=True)]
    all_to_all x2 -> x0, blocking collectives: 46.6 us -> none  [the longest x1 25.4 us: attend(): return lax.all_to_all(out, CTX, split_axis=1, concat_axis=2, tiled=True)]
    all_to_all x3 -> x0, starting transfers between devices: 28.8 us -> none  [the longest x1 17.6 us: on_device(): lax.all_to_all(qkv, CTX, split_axis=2, concat_axis=1, tiled=True)]
    slice x4 -> x0, local copies, waits for them, and re-layouts: 17.3 us -> none  [the longest x2 15.2 us: on_device(): padded[2 - lag:2 - lag + f_dev, row:row + height, col:col + width, :]]
    reshape x4 -> x0, local copies, waits for them, and re-layouts: 13.7 us -> none  [the longest x2 11.9 us: on_device(): qkv.astype(jnp.bfloat16)]
  transfers between devices with their start and end apart: 6 -> 0, of which waited for: 4 -> 0; matrix products, arithmetic and copies ran while one was open for 27% -> 0% of each run, Pallas kernels for 0% -> 0%
where the time goes in v1:
time: 155 us
  Pallas kernels  149 us (96%)
  local copies, waits for them, and re-layouts  4.69 us (3%)
    pallas_call x1, Pallas kernels, sections(): pl.pallas_call(section_kernel, out_shape=(jax.ShapeDtypeStruct((5, 256, 5...  103 us
    pallas_call x1, Pallas kernels, attention(): pl.pallas_call(attention_kernel, out_shape=jax.ShapeDtypeStruct((320, 153...  45.9 us

profile of v1, /device:TPU:1, one launch (start us, length us, event | category | flops | bytes accessed | tf_op | source)
XLA Modules:
  0.0 154.7 jit_solution(14901089850874791134)
XLA Ops:
  1.3 0.7 tile.4
  2.0 0.8 copy.11.lw4
  2.8 102.8 %sections.1 = (bf16[5,256,512]{2,1,0:T(8,128)(2,1)}, bf16[2,2,4,4,96,1152]{5,4,3,2,1,0:T(8,128)(2,1)}, bf16[32,5,48,128]{3,2,1,0:T(8,128)(2,1)}) custom-call(bf16[5,256,512]{2,1,0:T(8,128)(2,1)} %bitcast.16, bf16[5,64,3072]{2,1,0:T(8,128)(2,1)} %bitcast.14, s32[1]{0:T(128)} %copy.14.length, bf16[9,1536,512]{2,1,0:T(8,128)(2,1)} %bitcast.12, ...), custom_call_target="tpu_custom_call" | custom-call | tf_op jit(solution)/shard_map/sections/pallas_call | solution.py:272
  105.5 0.6 broadcast_in_dim.3.lens
  106.1 0.0 copy-start.1
  106.1 45.9 %attention.1 = bf16[320,1536]{1,0:T(8,128)(2,1)} custom-call(bf16[2,3072,1152]{2,1,0:T(8,128)(2,1)} %bitcast.11, bf16[7680,128]{1,0:T(8,128)(2,1)} %bitcast.15, s32[8,128]{1,0:T(8,128)} %broadcast_in_dim.3.lens), custom_call_target="tpu_custom_call" | custom-call | tf_op jit(solution)/shard_map/attention/pallas_call | solution.py:429
  152.1 0.0 copy-start
  152.1 0.0 copy-done.1
  152.1 1.1 copy.15
  153.2 0.6 copy-done
  153.8 0.9 copy.16
Async XLA Ops:
  106.1 46.0 %copy-start.1 = (bf16[5,256,512]{2,1,0:T(8,128)(2,1)S(1)}, bf16[5,256,512]{2,1,0:T(8,128)(2,1)}, u32[]{:S(2)}) copy-start(bf16[5,256,512]{2,1,0:T(8,128)(2,1)} %get-tuple-element.5) | copy-start | bytes 3932164
  152.1 1.7 %copy-start = (bf16[320,1536]{1,0:T(8,128)(2,1)S(1)}, bf16[320,1536]{1,0:T(8,128)(2,1)}, u32[]{:S(2)}) copy-start(bf16[320,1536]{1,0:T(8,128)(2,1)} %attention.1) | copy-start | bytes 2949124

commit v2 on v1

v2 whole, which is shorter than its diff:
```python
import jax
import jax.numpy as jnp
from jax import lax
from jax.experimental import pallas as pl
from jax.experimental.pallas import tpu as pltpu
from jax.sharding import Mesh
from jax.sharding import PartitionSpec as P

AXES = ("xl", "co", "xh", "y", "z")
CTX = ("xh", "y", "z")
MESH = pl.DeviceIdType.MESH
F32 = jnp.float32
BF16 = jnp.bfloat16
NCTX = 32
LANES = 128


def place():
    return {a: lax.axis_index(a) for a in AXES}


def ctx_of(me):
    return (me["xh"] * 4 + me["y"]) * 4 + me["z"]


def at_ctx(me, c, co=None):
    return (me["xl"], me["co"] if co is None else co, c // 16, (c // 4) % 4, c % 4)


def coordinate(me, axis):
    return (me["xh"] * 2 + me["xl"], me["y"], me["z"])[axis]


def moved(me, axis, c):
    if axis == 0:
        return (c % 2, me["co"], c // 2, me["y"], me["z"])
    if axis == 1:
        return (me["xl"], me["co"], me["xh"], c, me["z"])
    return (me["xl"], me["co"], me["xh"], me["y"], c)


def gather_copies(me, wall, ssem, rsem, r):
    rows = wall.shape[5] // 3
    half = rows // 2
    stages = [[] for _ in range(6)]
    for part in range(3):
        for phase in range(3):
            axis = (part + phase) % 3
            full = [(part + i) % 3 for i in range(phase)]
            c = coordinate(me, axis)
            for step in range(2):
                for way in range(2):
                    sign = 1 - 2 * way
                    to = (c + sign + 4) % 4
                    held = c if step == 0 else (c - sign + 4) % 4
                    begin = part * rows + (half if step and way else 0)
                    size = half if step else rows
                    index = [r]
                    for a in range(3):
                        if a in full:
                            got = None
                        elif a == axis:
                            got = held
                        else:
                            got = coordinate(me, a)
                        if a == 0:
                            if got is None:
                                index += [pl.ds(0, 2), pl.ds(0, 2)]
                            else:
                                index += [got % 2, got // 2]
                        else:
                            index.append(pl.ds(0, 4) if got is None else got)
                    block = wall.at[(*index, pl.ds(begin, size))]
                    n = (((r * 3 + part) * 3 + phase) * 2 + step) * 2 + way
                    stages[phase * 2 + step].append(
                        pltpu.make_async_remote_copy(
                            src_ref=block,
                            dst_ref=block,
                            send_sem=ssem.at[n],
                            recv_sem=rsem.at[n],
                            device_id=moved(me, axis, to),
                            device_id_type=MESH,
                        )
                    )
    return stages


TICKS = (
    ((0, 0),),
    ((0, 1),),
    ((0, 2), (1, 0)),
    ((0, 3), (1, 1)),
    ((0, 4), (1, 2)),
    ((0, 5), (1, 3), (2, 0)),
    ((1, 4), (2, 1)),
    ((1, 5), (2, 2)),
    ((2, 3),),
    ((2, 4),),
    ((2, 5),),
)


def block_kernel(
    frames, stream, length, lens, cw, lw4, ew, gain, w,
    sec_out, out,
    xin, xcat, cwv, acc, secb, strm, nt, sb, sent, wall, xr, xs, lboth, xf, xm, qs, of, osd, osent, orr,
    cw_sem, in_sem, w_ssem, w_rsem, h_ssem, h_rsem, a_ssem, a_rsem, out_sem, own_sem,
    x_ssem, x_rsem, o_ssem, o_rsem, o_own,
):
    me = place()
    ctx = ctx_of(me)
    co = me["co"]
    place_w = [
        pltpu.make_async_copy(
            w.at[:, pl.ds(384 * r, 384)],
            wall.at[r, me["xl"], me["xh"], me["y"], me["z"]],
            own_sem.at[5 + r],
        )
        for r in range(3)
    ]
    for copy in place_w:
        copy.start()
    load_frames = pltpu.make_async_copy(frames, xin.at[pl.ds(2, 5)], in_sem.at[0])
    load_frames.start()

    def order(n):
        k = n % 9
        return (2 - k // 3) * 3 + k % 3

    def load_cw(n):
        return pltpu.make_async_copy(cw.at[order(n)], cwv.at[n % 4], cw_sem.at[n % 4])

    for n in range(3):
        load_cw(n).start()
    load_stream = pltpu.make_async_copy(stream, strm, in_sem.at[1])
    load_stream.start()

    barrier = pltpu.get_barrier_semaphore()

    @pl.loop(1, NCTX)
    def _(k):
        pl.semaphore_signal(
            barrier, inc=1, device_id=at_ctx(me, (ctx + k) % NCTX), device_id_type=MESH
        )

    @pl.loop(0, NCTX)
    def _(k):
        pl.semaphore_signal(
            barrier, inc=1, device_id=at_ctx(me, (ctx + k) % NCTX, 1 - co), device_id_type=MESH
        )

    x = coordinate(me, 0)
    for d in (1, 3):
        pl.semaphore_signal(
            barrier, inc=1, device_id=moved(me, 0, (x + d) % 4), device_id_type=MESH
        )
    pl.semaphore_wait(barrier, 2 * NCTX + 1)

    halo = pltpu.make_async_remote_copy(
        src_ref=frames.at[pl.ds(3, 2)],
        dst_ref=xin.at[pl.ds(0, 2)],
        send_sem=h_ssem,
        recv_sem=h_rsem,
        device_id=at_ctx(me, (ctx + 1) % NCTX),
        device_id_type=MESH,
    )
    halo.start()
    for copy in place_w:
        copy.wait()
    rounds = [gather_copies(me, wall, w_ssem, w_rsem, r) for r in range(3)]

    def tick(n):
        for r, stage in TICKS[n]:
            if stage:
                for copy in rounds[r][stage - 1]:
                    copy.wait_recv()
            for copy in rounds[r][stage]:
                copy.start()

    tick(0)

    edge = jnp.zeros((7, 1, 16, 1536), BF16)
    xcat[:, pl.ds(0, 1)] = edge
    xcat[:, pl.ds(17, 1)] = edge
    column = lax.broadcasted_iota(jnp.int32, (256, 512), 0) & 15

    def spread(i, factor):
        v = xin[i].astype(F32)
        act = (v / (1.0 + jnp.exp(-v))).astype(BF16).astype(F32) * factor
        before = jnp.where(column == 0, 0.0, pltpu.roll(act, 1, 0))
        after = jnp.where(column == 15, 0.0, pltpu.roll(act, 255, 0))
        for b, part in enumerate((before, act, after)):
            xcat[i, pl.ds(1, 16), :, pl.ds(512 * b, 512)] = part.astype(BF16).reshape(16, 16, 512)

    load_frames.wait()

    @pl.loop(2, 7)
    def _(i):
        spread(i, 1.0)

    tick(1)
    cell = lax.broadcasted_iota(jnp.int32, (256, 64), 0)
    lane = lax.broadcasted_iota(jnp.int32, (256, 64), 1)
    corner = ((cell >> 4) & 1) * 2 + (cell & 1)
    keep = jnp.where((lane >> 4) == corner, 1.0, 0.0)
    tok = lax.broadcasted_iota(jnp.int32, (64, 256), 0)
    cel = lax.broadcasted_iota(jnp.int32, (64, 256), 1)
    pick = jnp.where((cel >> 5) * 8 + ((cel & 15) >> 1) == tok, 1.0, 0.0).astype(BF16)
    count = length[0]

    def conv(first, many, checkpoints, begin):
        acc[pl.ds(0, many * 256)] = jnp.zeros((many * 256, 512), F32)

        @pl.loop(0, 9)
        def _(k):
            n = begin + k
            load_cw(n).wait()

            @pl.when(n < 15)
            def _():
                load_cw(n + 3).start()

            for when, now in checkpoints:
                @pl.when(k == when)
                def _():
                    tick(now)

            @pl.when(k == 6)
            def _():
                for f in range(many):
                    video = jnp.where(ctx * 5 + first + f < count, 1.0, 0.0)
                    acc[pl.ds(f * 256, 256)] = acc[pl.ds(f * 256, 256)] * video

            lag = 2 - k // 3
            slab = xcat[pl.ds(first + 2 - lag, many), pl.ds(k % 3, 16)]
            acc[pl.ds(0, many * 256)] += jnp.dot(
                slab.reshape(many * 256, 1536), cwv[n % 4], preferred_element_type=F32
            )

    def finish(first, many, n):
        @pl.loop(0, many)
        def _(i):
            t = first + i
            sec = (xin[t + 2].astype(F32) + acc[pl.ds(pl.multiple_of(i * 256, 256), 256)]).astype(BF16)
            secb[t] = sec
            lat = jnp.dot(sec, lw4[...], preferred_element_type=F32).astype(BF16).astype(F32)
            patches = jnp.dot(pick, (lat * keep).astype(BF16), preferred_element_type=F32).astype(BF16)
            e = jnp.dot(patches, ew[...], preferred_element_type=F32) + strm[t].astype(F32)
            scale = lax.rsqrt(jnp.mean(e * e, axis=-1, keepdims=True) + 1e-06)
            e = e * scale * gain[...]
            for j in range(24):
                nt[pl.ds(j, 64, stride=24), :] = e[:, j * LANES : (j + 1) * LANES]
            sb[t] = nt[...].astype(BF16).reshape(32, 48, LANES)

        span = pl.ds(first, many)
        pltpu.make_async_copy(secb.at[span], sec_out.at[span], out_sem.at[n]).start()
        stage = pltpu.make_async_copy(sb.at[span], sent.at[span], own_sem.at[1 + n])
        stage.start()
        stage.wait()

        @pl.loop(1, NCTX)
        def _(k):
            to = (ctx + k) % NCTX
            pltpu.make_async_remote_copy(
                src_ref=sent.at[span, to],
                dst_ref=xr.at[ctx, span],
                send_sem=a_ssem.at[n],
                recv_sem=a_rsem.at[n],
                device_id=at_ctx(me, to),
                device_id_type=MESH,
            ).start()

        pltpu.make_async_copy(sent.at[span, ctx], xr.at[ctx, span], own_sem.at[3 + n]).start()

    conv(2, 3, ((1, 2), (4, 3), (8, 4)), 0)
    load_stream.wait()
    finish(2, 3, 0)
    tick(5)
    halo.wait_recv()
    inner = jnp.where(ctx > 0, 1.0, 0.0)

    @pl.loop(0, 2)
    def _(i):
        spread(i, inner)

    conv(0, 2, ((5, 6),), 9)
    finish(0, 2, 1)
    tick(7)

    for n, (first, many) in enumerate(((2, 3), (0, 2))):
        span = pl.ds(first, many)
        bulk = xr.at[pl.ds(0, NCTX - 1), span]
        pltpu.make_async_copy(bulk, bulk, a_rsem.at[n]).wait()
        pltpu.make_async_copy(sent.at[span, ctx], xr.at[ctx, span], own_sem.at[3 + n]).wait()
    swaps = [
        pltpu.make_async_remote_copy(
            src_ref=a,
            dst_ref=b,
            send_sem=x_ssem.at[n],
            recv_sem=x_rsem.at[n],
            device_id=at_ctx(me, ctx, 1 - co),
            device_id_type=MESH,
        )
        for n, (a, b) in enumerate(((xr, xs), (lens, lboth.at[1])))
    ]
    for copy in swaps:
        copy.start()
    tick(8)
    lboth[0] = lens[...]

    def fill(g, src):
        xf[...] = src[...].astype(F32).reshape(7680, LANES)
        for f in range(5):
            for pos in range(2):
                for j in range(24):
                    xm[g, pl.ds(pos * 160 + f * 32, 32), pl.ds(j * LANES, LANES)] = xf[
                        pl.ds((f * 2 + pos) * 24 + j, 32, stride=240), :
                    ].astype(BF16)

    fill(0, xr)
    tick(9)
    for copy in swaps:
        copy.wait_recv()
    fill(1, xs)
    for copy in rounds[0][5]:
        copy.wait_recv()

    row = lax.broadcasted_iota(jnp.int32, (160, 160), 0)
    col = lax.broadcasted_iota(jnp.int32, (160, 160), 1)
    row_frame = (row & 31) * 5 + (row >> 5)
    col_frame = (col & 31) * 5 + (col >> 5)
    same = row == col

    def returned(r, g, to):
        return pltpu.make_async_remote_copy(
            src_ref=osent.at[r, g, to],
            dst_ref=orr.at[r, co, ctx],
            send_sem=o_ssem.at[r * 2 + g],
            recv_sem=o_rsem.at[r * 2 + g],
            device_id=at_ctx(me, to, co if g == 0 else 1 - co),
            device_id_type=MESH,
        )

    def kept(r):
        return pltpu.make_async_copy(osent.at[r, 0, ctx], orr.at[r, co, ctx], o_own.at[r])

    @pl.loop(0, 3)
    def _(r):
        @pl.when(r == 1)
        def _():
            tick(10)
            for copy in rounds[1][5]:
                copy.wait_recv()

        @pl.when(r == 2)
        def _():
            for copy in rounds[2][5]:
                copy.wait_recv()

        @pl.loop(0, 4)
        def _(q):
            g = q // 2
            hq = q % 2
            qs[...] = jnp.dot(
                xm[g], wall[r, hq].reshape(3072, 384), preferred_element_type=F32
            ).astype(BF16)
            most = jnp.broadcast_to(lboth[g, 0:1, 0:1], (160, 160))
            allowed = ((row_frame < most) & (col_frame < most)) | same
            for pos in range(2):
                rows = pl.ds(pos * 160, 160)
                scores = lax.dot_general(
                    qs[rows, 0:128], qs[rows, 128:256], (((1,), (1,)), ((), ())),
                    preferred_element_type=F32,
                ) * (128.0 ** -0.5)
                scores = jnp.where(allowed, scores, -1e30)
                expo = jnp.exp(scores - jnp.max(scores, axis=-1, keepdims=True))
                probs = (expo / jnp.sum(expo, axis=-1, keepdims=True)).astype(BF16)
                o = jnp.dot(probs, qs[rows, 256:384], preferred_element_type=F32)
                for f in range(5):
                    of[pl.ds(g * 768 + f * 4 + pos * 2 + hq, 32, stride=24), :] = o[
                        f * 32 : (f + 1) * 32
                    ]

        osd[r] = of[...].astype(BF16).reshape(2, NCTX, 24, LANES)
        stage = pltpu.make_async_copy(osd.at[r], osent.at[r], own_sem.at[0])
        stage.start()
        stage.wait()

        @pl.loop(1, NCTX)
        def _(k):
            returned(r, 0, (ctx + k) % NCTX).start()

        @pl.loop(0, NCTX)
        def _(k):
            returned(r, 1, (ctx + k) % NCTX).start()

        kept(r).start()

    for stages in rounds:
        for stage in stages:
            for copy in stage:
                copy.wait_send()
    halo.wait_send()
    for copy in swaps:
        copy.wait_send()
    for n, (first, many) in enumerate(((2, 3), (0, 2))):
        span = pl.ds(first, many)
        bulk = xr.at[pl.ds(0, NCTX - 1), span]
        pltpu.make_async_copy(bulk, bulk, a_ssem.at[n]).wait()
        pltpu.make_async_copy(secb.at[span], sec_out.at[span], out_sem.at[n]).wait()
    for r in range(3):
        kept(r).wait()
        for g in range(2):
            bulk = orr.at[0, 0, pl.ds(0, NCTX - 1 + g)]
            pltpu.make_async_copy(bulk, bulk, o_rsem.at[r * 2 + g]).wait()
            pltpu.make_async_copy(bulk, bulk, o_ssem.at[r * 2 + g]).wait()
    xf[pl.ds(0, 4608)] = orr[...].astype(F32).reshape(4608, LANES)
    for r in range(3):
        for c in range(2):
            for hq in range(2):
                head = 6 * hq + 3 * c + r
                for f in range(5):
                    for pos in range(2):
                        xf[pl.ds(4608 + f * 64 + pos, 32, stride=2), :] = xf[
                            pl.ds((r * 2 + c) * 768 + f * 4 + pos * 2 + hq, 32, stride=24), :
                        ]
                out[:, pl.ds(head * LANES, LANES)] = xf[pl.ds(4608, 320)].astype(BF16)


def block(frames, stream, length, lens, cw, lw4, ew, gain, w):
    hbm = pl.BlockSpec(memory_space=pl.ANY)
    vmem = pl.BlockSpec(memory_space=pltpu.VMEM)
    smem = pl.BlockSpec(memory_space=pltpu.SMEM)
    dma = pltpu.SemaphoreType.DMA
    return pl.pallas_call(
        block_kernel,
        out_shape=(
            jax.ShapeDtypeStruct((5, 256, 512), BF16),
            jax.ShapeDtypeStruct((320, 1536), BF16),
        ),
        in_specs=[hbm, hbm, smem, vmem, hbm, vmem, vmem, vmem, vmem],
        out_specs=(hbm, vmem),
        scratch_shapes=[
            pltpu.VMEM((7, 256, 512), BF16),
            pltpu.VMEM((7, 18, 16, 1536), BF16),
            pltpu.VMEM((4, 1536, 512), BF16),
            pltpu.VMEM((768, 512), F32),
            pltpu.VMEM((5, 256, 512), BF16),
            pltpu.VMEM((5, 64, 3072), BF16),
            pltpu.VMEM((1536, LANES), F32),
            pltpu.VMEM((5, 32, 48, LANES), BF16),
            pltpu.VMEM((5, 32, 48, LANES), BF16),
            pltpu.VMEM((3, 2, 2, 4, 4, 96, 384), BF16),
            pltpu.VMEM((NCTX, 5, 48, LANES), BF16),
            pltpu.VMEM((NCTX, 5, 48, LANES), BF16),
            pltpu.VMEM((2, 8, LANES), jnp.int32),
            pltpu.VMEM((7680, LANES), F32),
            pltpu.VMEM((2, 320, 3072), BF16),
            pltpu.VMEM((320, 384), BF16),
            pltpu.VMEM((1536, LANES), F32),
            pltpu.VMEM((3, 2, NCTX, 24, LANES), BF16),
            pltpu.VMEM((3, 2, NCTX, 24, LANES), BF16),
            pltpu.VMEM((3, 2, NCTX, 24, LANES), BF16),
            dma((4,)), dma((2,)), dma((108,)), dma((108,)), dma, dma, dma((2,)), dma((2,)), dma((2,)), dma((8,)),
            dma((2,)), dma((2,)), dma((6,)), dma((6,)), dma((3,)),
        ],
        compiler_params=pltpu.CompilerParams(
            collective_id=0, has_side_effects=True, vmem_limit_bytes=63 * 2**20
        ),
        name="block",
    )(frames, stream, length, lens, cw, lw4, ew, gain, w)


def on_device(frames, stream, video_frames, conv_weight, latent_weight, embed_weight, norm_gain, qkv_weight):
    section, mixed = block(
        frames.reshape(5, 256, 512),
        stream.reshape(5, 64, 3072),
        video_frames,
        jnp.broadcast_to(video_frames[0], (8, LANES)),
        conv_weight.reshape(9, 1536, 512),
        jnp.tile(latent_weight, (1, 4)),
        embed_weight,
        norm_gain.reshape(1, 3072),
        qkv_weight,
    )
    return section.reshape(frames.shape), mixed.reshape(1, 5, 64, 1536)


def solution(mesh):
    finer = Mesh(mesh.devices.reshape(2, 2, 2, 4, 4), AXES)
    dp = ("xl", "co")
    return jax.shard_map(
        on_device,
        mesh=finer,
        in_specs=(
            P(dp, CTX, None, None, None),
            P(dp, CTX, None, None),
            P(dp),
            P(),
            P(),
            P(),
            P(),
            P(CTX, dp),
        ),
        out_specs=(P(dp, CTX, None, None, None), P(dp, CTX, None, None)),
        check_vma=False,
    )
```

time: 155 us -> 147 us (0.948)
  Pallas kernels: 149 us -> 139 us
    pallas_call x2 -> x1, Pallas kernels: 149 us -> 139 us  [block(): pl.pallas_call(block_kernel, out_shape=(jax.ShapeDtypeStruct((5, 256, 512...]
    unnamed x6 -> x4, local copies, waits for them, and re-layouts: 2.6 us -> 3.55 us
where the time goes in v2:
time: 147 us; the launch traced here: 146 us
  Pallas kernels  139 us (95%)
  local copies, waits for them, and re-layouts  5.63 us (4%)
    pallas_call x1, Pallas kernels, block(): pl.pallas_call(block_kernel, out_shape=(jax.ShapeDtypeStruct((5, 256, 512...  139 us
    unnamed x4, local copies, waits for them, and re-layouts  3.55 us

profile of v2, /device:TPU:1, one launch (start us, length us, event | category | flops | bytes accessed | tf_op | source)
XLA Modules:
  0.0 146.3 jit_solution(4545363815837087577)
XLA Ops:
  1.3 0.6 broadcast_in_dim.3.lens
  1.9 0.7 tile.4
  2.6 0.8 copy.11.lw4
  3.4 139.4 %block.1 = (bf16[5,256,512]{2,1,0:T(8,128)(2,1)}, bf16[320,1536]{1,0:T(8,128)(2,1)}) custom-call(bf16[5,256,512]{2,1,0:T(8,128)(2,1)} %bitcast.11, bf16[5,64,3072]{2,1,0:T(8,128)(2,1)} %bitcast.10, s32[1]{0:T(128)} %copy.14.length, s32[8,128]{1,0:T(8,128)} %broadcast_in_dim.3.lens, bf16[9,1536,512]{2,1,0:T(8,128)(2,1)} %bitcast.9, ...), custom_call_target="tpu_custom_call" | custom-call | tf_op jit(solution)/shard_map/block/pallas_call | solution.py:435
  142.8 0.0 copy-start
  142.8 2.6 %copy.15 = bf16[1,5,16,16,512]{4,3,2,1,0:T(8,128)(2,1)} copy(bf16[1,5,16,16,512]{4,3,2,1,0:T(8,128)(2,1)} %bitcast.12) | data formatting | bytes 2621440
  145.4 0.0 copy-done
  145.4 0.9 copy.16
Async XLA Ops:
  142.8 2.6 %copy-start = (bf16[320,1536]{1,0:T(8,128)(2,1)S(1)}, bf16[320,1536]{1,0:T(8,128)(2,1)}, u32[]{:S(2)}) copy-start(bf16[320,1536]{1,0:T(8,128)(2,1)} %get-tuple-element.5) | copy-start | bytes 2949124

commit v3 on v2

--- a/solution.py
+++ b/solution.py
@@ -41,7 +41,6 @@
 
 def gather_copies(me, wall, ssem, rsem, r):
     rows = wall.shape[5] // 3
-    half = rows // 2
     stages = [[] for _ in range(6)]
     for part in range(3):
         for phase in range(3):
@@ -53,8 +52,9 @@
                     sign = 1 - 2 * way
                     to = (c + sign + 4) % 4
                     held = c if step == 0 else (c - sign + 4) % 4
-                    begin = part * rows + (half if step and way else 0)
-                    size = half if step else rows
+                    cut = rows // 2
+                    begin = part * rows + (cut if step and way else 0)
+                    size = rows if not step else rows - cut if way else cut
                     index = [r]
                     for a in range(3):
                         if a in full:
@@ -86,22 +86,18 @@
 
 
 TICKS = (
-    ((0, 0),),
-    ((0, 1),),
-    ((0, 2), (1, 0)),
-    ((0, 3), (1, 1)),
-    ((0, 4), (1, 2)),
-    ((0, 5), (1, 3), (2, 0)),
-    ((1, 4), (2, 1)),
-    ((1, 5), (2, 2)),
-    ((2, 3),),
-    ((2, 4),),
+    ((0, 0), (1, 0), (2, 0)),
+    ((0, 1), (1, 1), (2, 1)),
+    ((0, 2), (1, 2), (2, 2)),
+    ((0, 3), (1, 3), (2, 3)),
+    ((0, 4), (1, 4)),
+    ((0, 5), (1, 5), (2, 4)),
     ((2, 5),),
 )
 
 
 def block_kernel(
-    frames, stream, length, lens, cw, lw4, ew, gain, w,
+    frames, stream, length, cw, lw, ew, gain, w,
     sec_out, out,
     xin, xcat, cwv, acc, secb, strm, nt, sb, sent, wall, xr, xs, lboth, xf, xm, qs, of, osd, osent, orr,
     cw_sem, in_sem, w_ssem, w_rsem, h_ssem, h_rsem, a_ssem, a_rsem, out_sem, own_sem,
@@ -110,6 +106,7 @@
     me = place()
     ctx = ctx_of(me)
     co = me["co"]
+    lboth[0] = jnp.full((8, LANES), length[0], jnp.int32)
     place_w = [
         pltpu.make_async_copy(
             w.at[:, pl.ds(384 * r, 384)],
@@ -165,6 +162,19 @@
         device_id_type=MESH,
     )
     halo.start()
+
+    def swap(n, a, b):
+        return pltpu.make_async_remote_copy(
+            src_ref=a,
+            dst_ref=b,
+            send_sem=x_ssem.at[n],
+            recv_sem=x_rsem.at[n],
+            device_id=at_ctx(me, ctx, 1 - co),
+            device_id_type=MESH,
+        )
+
+    swap_lens = swap(2, lboth.at[0], lboth.at[1])
+    swap_lens.start()
     for copy in place_w:
         copy.wait()
     rounds = [gather_copies(me, wall, w_ssem, w_rsem, r) for r in range(3)]
@@ -206,6 +216,9 @@
     tok = lax.broadcasted_iota(jnp.int32, (64, 256), 0)
     cel = lax.broadcasted_iota(jnp.int32, (64, 256), 1)
     pick = jnp.where((cel >> 5) * 8 + ((cel & 15) >> 1) == tok, 1.0, 0.0).astype(BF16)
+    source = lax.broadcasted_iota(jnp.int32, (16, 64), 0)
+    target = lax.broadcasted_iota(jnp.int32, (16, 64), 1)
+    copies = jnp.where((target & 15) == source, 1.0, 0.0).astype(BF16)
     count = length[0]
 
     def conv(first, many, checkpoints, begin):
@@ -243,7 +256,10 @@
             t = first + i
             sec = (xin[t + 2].astype(F32) + acc[pl.ds(pl.multiple_of(i * 256, 256), 256)]).astype(BF16)
             secb[t] = sec
-            lat = jnp.dot(sec, lw4[...], preferred_element_type=F32).astype(BF16).astype(F32)
+            lat = lax.dot_general(
+                sec, lw[...], (((1,), (1,)), ((), ())), preferred_element_type=F32
+            ).astype(BF16)
+            lat = jnp.dot(lat, copies, preferred_element_type=F32)
             patches = jnp.dot(pick, (lat * keep).astype(BF16), preferred_element_type=F32).astype(BF16)
             e = jnp.dot(patches, ew[...], preferred_element_type=F32) + strm[t].astype(F32)
             scale = lax.rsqrt(jnp.mean(e * e, axis=-1, keepdims=True) + 1e-06)
@@ -272,10 +288,9 @@
 
         pltpu.make_async_copy(sent.at[span, ctx], xr.at[ctx, span], own_sem.at[3 + n]).start()
 
-    conv(2, 3, ((1, 2), (4, 3), (8, 4)), 0)
+    conv(2, 3, ((1, 2), (5, 3), (8, 4)), 0)
     load_stream.wait()
     finish(2, 3, 0)
-    tick(5)
     halo.wait_recv()
     inner = jnp.where(ctx > 0, 1.0, 0.0)
 
@@ -283,30 +298,17 @@
     def _(i):
         spread(i, inner)
 
-    conv(0, 2, ((5, 6),), 9)
+    conv(0, 2, (), 9)
     finish(0, 2, 1)
-    tick(7)
-
+    tick(5)
+    swaps = []
     for n, (first, many) in enumerate(((2, 3), (0, 2))):
         span = pl.ds(first, many)
         bulk = xr.at[pl.ds(0, NCTX - 1), span]
         pltpu.make_async_copy(bulk, bulk, a_rsem.at[n]).wait()
         pltpu.make_async_copy(sent.at[span, ctx], xr.at[ctx, span], own_sem.at[3 + n]).wait()
-    swaps = [
-        pltpu.make_async_remote_copy(
-            src_ref=a,
-            dst_ref=b,
-            send_sem=x_ssem.at[n],
-            recv_sem=x_rsem.at[n],
-            device_id=at_ctx(me, ctx, 1 - co),
-            device_id_type=MESH,
-        )
-        for n, (a, b) in enumerate(((xr, xs), (lens, lboth.at[1])))
-    ]
-    for copy in swaps:
-        copy.start()
-    tick(8)
-    lboth[0] = lens[...]
+        swaps.append(swap(n, xr.at[:, span], xs.at[:, span]))
+        swaps[-1].start()
 
     def fill(g, src):
         xf[...] = src[...].astype(F32).reshape(7680, LANES)
@@ -318,10 +320,6 @@
                     ].astype(BF16)
 
     fill(0, xr)
-    tick(9)
-    for copy in swaps:
-        copy.wait_recv()
-    fill(1, xs)
     for copy in rounds[0][5]:
         copy.wait_recv()
 
@@ -348,7 +346,7 @@
     def _(r):
         @pl.when(r == 1)
         def _():
-            tick(10)
+            tick(6)
             for copy in rounds[1][5]:
                 copy.wait_recv()
 
@@ -359,6 +357,13 @@
 
         @pl.loop(0, 4)
         def _(q):
+            @pl.when(r * 4 + q == 2)
+            def _():
+                swap_lens.wait_recv()
+                for copy in swaps:
+                    copy.wait_recv()
+                fill(1, xs)
+
             g = q // 2
             hq = q % 2
             qs[...] = jnp.dot(
@@ -401,6 +406,7 @@
             for copy in stage:
                 copy.wait_send()
     halo.wait_send()
+    swap_lens.wait_send()
     for copy in swaps:
         copy.wait_send()
     for n, (first, many) in enumerate(((2, 3), (0, 2))):
@@ -413,21 +419,24 @@
         for g in range(2):
             bulk = orr.at[0, 0, pl.ds(0, NCTX - 1 + g)]
             pltpu.make_async_copy(bulk, bulk, o_rsem.at[r * 2 + g]).wait()
-            pltpu.make_async_copy(bulk, bulk, o_ssem.at[r * 2 + g]).wait()
-    xf[pl.ds(0, 4608)] = orr[...].astype(F32).reshape(4608, LANES)
-    for r in range(3):
+        xf[pl.ds(0, 1536)] = orr[r].astype(F32).reshape(1536, LANES)
         for c in range(2):
             for hq in range(2):
                 head = 6 * hq + 3 * c + r
+                base = 1536 + 320 * (r * 4 + c * 2 + hq)
                 for f in range(5):
                     for pos in range(2):
-                        xf[pl.ds(4608 + f * 64 + pos, 32, stride=2), :] = xf[
-                            pl.ds((r * 2 + c) * 768 + f * 4 + pos * 2 + hq, 32, stride=24), :
+                        xf[pl.ds(base + f * 64 + pos, 32, stride=2), :] = xf[
+                            pl.ds(c * 768 + f * 4 + pos * 2 + hq, 32, stride=24), :
                         ]
-                out[:, pl.ds(head * LANES, LANES)] = xf[pl.ds(4608, 320)].astype(BF16)
-
-
-def block(frames, stream, length, lens, cw, lw4, ew, gain, w):
+                out[:, pl.ds(head * LANES, LANES)] = xf[pl.ds(base, 320)].astype(BF16)
+    for r in range(3):
+        for g in range(2):
+            bulk = orr.at[0, 0, pl.ds(0, NCTX - 1 + g)]
+            pltpu.make_async_copy(bulk, bulk, o_ssem.at[r * 2 + g]).wait()
+
+
+def block(frames, stream, length, cw, lw, ew, gain, w):
     hbm = pl.BlockSpec(memory_space=pl.ANY)
     vmem = pl.BlockSpec(memory_space=pltpu.VMEM)
     smem = pl.BlockSpec(memory_space=pltpu.SMEM)
@@ -438,7 +447,7 @@
             jax.ShapeDtypeStruct((5, 256, 512), BF16),
             jax.ShapeDtypeStruct((320, 1536), BF16),
         ),
-        in_specs=[hbm, hbm, smem, vmem, hbm, vmem, vmem, vmem, vmem],
+        in_specs=[hbm, hbm, smem, hbm, vmem, vmem, vmem, vmem],
         out_specs=(hbm, vmem),
         scratch_shapes=[
             pltpu.VMEM((7, 256, 512), BF16),
@@ -462,13 +471,13 @@
             pltpu.VMEM((3, 2, NCTX, 24, LANES), BF16),
             pltpu.VMEM((3, 2, NCTX, 24, LANES), BF16),
             dma((4,)), dma((2,)), dma((108,)), dma((108,)), dma, dma, dma((2,)), dma((2,)), dma((2,)), dma((8,)),
-            dma((2,)), dma((2,)), dma((6,)), dma((6,)), dma((3,)),
+            dma((3,)), dma((3,)), dma((6,)), dma((6,)), dma((3,)),
         ],
         compiler_params=pltpu.CompilerParams(
             collective_id=0, has_side_effects=True, vmem_limit_bytes=63 * 2**20
         ),
         name="block",
-    )(frames, stream, length, lens, cw, lw4, ew, gain, w)
+    )(frames, stream, length, cw, lw, ew, gain, w)
 
 
 def on_device(frames, stream, video_frames, conv_weight, latent_weight, embed_weight, norm_gain, qkv_weight):
@@ -476,9 +485,8 @@
         frames.reshape(5, 256, 512),
         stream.reshape(5, 64, 3072),
         video_frames,
-        jnp.broadcast_to(video_frames[0], (8, LANES)),
         conv_weight.reshape(9, 1536, 512),
-        jnp.tile(latent_weight, (1, 4)),
+        latent_weight.T,
         embed_weight,
         norm_gain.reshape(1, 3072),
         qkv_weight,

time: 147 us -> 134 us (0.912)
  Pallas kernels: 139 us -> 129 us
  local copies, waits for them, and re-layouts: 5.63 us -> 3.55 us
    pallas_call x1, Pallas kernels: 139 us -> 129 us  [block(): pl.pallas_call(block_kernel, out_shape=(jax.ShapeDtypeStruct((5, 256, 512...]
    another operation x2 -> x0, local copies, waits for them, and re-layouts: 1.48 us -> none  [on_device(): jnp.tile(latent_weight, (1, 4))]
where the time goes in v3:
time: 134 us
  Pallas kernels  129 us (96%)
  local copies, waits for them, and re-layouts  3.55 us (3%)
    pallas_call x1, Pallas kernels, block(): pl.pallas_call(block_kernel, out_shape=(jax.ShapeDtypeStruct((5, 256, 512...  129 us
    unnamed x4, local copies, waits for them, and re-layouts  3.55 us

profile of v3, /device:TPU:1, one launch (start us, length us, event | category | flops | bytes accessed | tf_op | source)
XLA Modules:
  0.0 134.3 jit_solution(10808628894589724714)
XLA Ops:
  1.3 129.5 %block.1 = (bf16[5,256,512]{2,1,0:T(8,128)(2,1)}, bf16[320,1536]{1,0:T(8,128)(2,1)}) custom-call(bf16[5,256,512]{2,1,0:T(8,128)(2,1)} %bitcast.9, bf16[5,64,3072]{2,1,0:T(8,128)(2,1)} %bitcast.8, s32[1]{0:T(128)S(6)} %copy.12.length, bf16[9,1536,512]{2,1,0:T(8,128)(2,1)} %bitcast.7, bf16[16,512]{1,0:T(8,128)(2,1)} %bitcast.12, bf16[64,3072]{1,0:T(8,128)(2,1)} %ew.1, ...), custom_call_target="tpu_custom_call" | custom-call | tf_op jit(solution)/shard_map/block/pallas_call | solution.py:444
  130.8 0.0 copy-start
  130.8 2.6 %copy.13 = bf16[1,5,16,16,512]{4,3,2,1,0:T(8,128)(2,1)} copy(bf16[1,5,16,16,512]{4,3,2,1,0:T(8,128)(2,1)} %bitcast.10) | data formatting | bytes 2621440
  133.4 0.0 copy-done
  133.4 0.9 copy.14
Async XLA Ops:
  130.8 2.6 %copy-start = (bf16[320,1536]{1,0:T(8,128)(2,1)S(1)}, bf16[320,1536]{1,0:T(8,128)(2,1)}, u32[]{:S(2)}) copy-start(bf16[320,1536]{1,0:T(8,128)(2,1)} %get-tuple-element.5) | copy-start | bytes 2949124

commit v4 on v3

--- a/solution.py
+++ b/solution.py
@@ -181,11 +181,15 @@
 
     def tick(n):
         for r, stage in TICKS[n]:
-            if stage:
-                for copy in rounds[r][stage - 1]:
-                    copy.wait_recv()
-            for copy in rounds[r][stage]:
-                copy.start()
+            phase = stage // 2
+            for axis in range(3):
+                part = (axis - phase) % 3
+                both = slice(2 * part, 2 * part + 2)
+                if stage:
+                    for copy in rounds[r][stage - 1][both]:
+                        copy.wait_recv()
+                for copy in rounds[r][stage][both]:
+                    copy.start()
 
     tick(0)
 
@@ -346,7 +350,6 @@
     def _(r):
         @pl.when(r == 1)
         def _():
-            tick(6)
             for copy in rounds[1][5]:
                 copy.wait_recv()
 
@@ -357,6 +360,10 @@
 
         @pl.loop(0, 4)
         def _(q):
+            @pl.when(r * 4 + q == 6)
+            def _():
+                tick(6)
+
             @pl.when(r * 4 + q == 2)
             def _():
                 swap_lens.wait_recv()

time: 134 us -> 134 us (level)
  no operation moved by 1% of the time
where the time goes in v4:
time: 134 us
  Pallas kernels  129 us (96%)
  local copies, waits for them, and re-layouts  3.55 us (3%)
    pallas_call x1, Pallas kernels, block(): pl.pallas_call(block_kernel, out_shape=(jax.ShapeDtypeStruct((5, 256, 512...  129 us
    unnamed x4, local copies, waits for them, and re-layouts  3.55 us

profile of v4, /device:TPU:1, one launch (start us, length us, event | category | flops | bytes accessed | tf_op | source)
XLA Modules:
  0.0 133.7 jit_solution(16000508104363553083)
XLA Ops:
  1.3 128.8 %block.1 = (bf16[5,256,512]{2,1,0:T(8,128)(2,1)}, bf16[320,1536]{1,0:T(8,128)(2,1)}) custom-call(bf16[5,256,512]{2,1,0:T(8,128)(2,1)} %bitcast.9, bf16[5,64,3072]{2,1,0:T(8,128)(2,1)} %bitcast.8, s32[1]{0:T(128)S(6)} %copy.12.length, bf16[9,1536,512]{2,1,0:T(8,128)(2,1)} %bitcast.7, bf16[16,512]{1,0:T(8,128)(2,1)} %bitcast.12, bf16[64,3072]{1,0:T(8,128)(2,1)} %ew.1, ...), custom_call_target="tpu_custom_call" | custom-call | tf_op jit(solution)/shard_map/block/pallas_call | solution.py:451
  130.1 0.0 copy-start
  130.1 2.6 %copy.13 = bf16[1,5,16,16,512]{4,3,2,1,0:T(8,128)(2,1)} copy(bf16[1,5,16,16,512]{4,3,2,1,0:T(8,128)(2,1)} %bitcast.10) | data formatting | bytes 2621440
  132.7 0.0 copy-done
  132.7 0.9 copy.14
Async XLA Ops:
  130.1 2.6 %copy-start = (bf16[320,1536]{1,0:T(8,128)(2,1)S(1)}, bf16[320,1536]{1,0:T(8,128)(2,1)}, u32[]{:S(2)}) copy-start(bf16[320,1536]{1,0:T(8,128)(2,1)} %get-tuple-element.5) | copy-start | bytes 2949124
